TPU v7x, 32 devices: a whole 2x2x4 slice. The times are simulated.
32 devices in a mesh: shard: 4 (over z), ctx: 2 (over y), tp: 4 (over x, core).
Axes of the slice: x: 2, y: 2, z: 4, core: 2. Of those that a mesh axis runs over, the one named last changes fastest.
Arguments:
- inputs: float32 [8, 256, 1024], P('shard', 'ctx'), may hold values from -12 to 12
- segment_ids: int32 [8, 256], P('shard', 'ctx'), may hold values from 0 to 3, never falling along the last dimension, each value on 1 to 128 neighbouring positions
- gains: bfloat16 [2, 1024], P(None, ('shard', 'ctx')), may hold values from 0.5 to 1.5
- shifts: bfloat16 [2, 1024], P(None, ('shard', 'ctx')), may hold values from -3 to 3
- attend_weight: bfloat16 [1024, 3, 1024], P(('shard', 'ctx'), None, 'tp'), may hold values from -1 to 1
- merge_weight: bfloat16 [1024, 1024], P(('shard', 'ctx'), 'tp'), may hold values from -0.75 to 0.75
- expand_weight: bfloat16 [1024, 4096], P(('shard', 'ctx'), 'tp'), may hold values from -0.1875 to 0.1875
- expand_bias: bfloat16 [4, 1024], P('tp', ('shard', 'ctx')), may hold values from -3 to 3
- reduce_weight: bfloat16 [1024, 4096], P(('shard', 'ctx'), 'tp'), may hold values from -0.09375 to 0.09375
- cotangent: float32 [8, 256, 1024], P('shard', 'ctx'), may hold values from -6 to 6
Outputs:
- block_out: float32 [8, 256, 1024], P('shard', 'ctx')
- input_grad: float32 [8, 256, 1024], P('shard', 'ctx')
- gains_grad: float32 [2, 1024], P(None, ('shard', 'ctx'))
- shifts_grad: float32 [2, 1024], P(None, ('shard', 'ctx'))
- attend_grad: float32 [1024, 3, 1024], P(('shard', 'ctx'), None, 'tp')
- merge_grad: float32 [1024, 1024], P(('shard', 'ctx'), 'tp')
- expand_grad: float32 [1024, 4096], P(('shard', 'ctx'), 'tp')
- bias_grad: float32 [4, 1024], P('tp', ('shard', 'ctx'))
- reduce_grad: float32 [1024, 4096], P(('shard', 'ctx'), 'tp')
Inputs may be any that keep to these rules, and one draw needn't show every extreme that they name: `segment_ids`: within each sequence segment ids never fall; every document holds 1 to 128 tokens, and one of them exactly 128.
All inputs are finite; a program needn't handle non-finite values.
Results may differ from a plain program's by a relative error of at most 0.0093.
Values may be sent and summed in bfloat16 or wider, within the bound.
No kernel may reach another device: no remote copies, remote signals or barrier semaphores. Data moves between devices by JAX's collectives and lax.ppermute only.
A program may use at most 128 MiB of HBM per device.

v0:
```python
import jax
import jax.numpy as jnp
from jax import lax
from jax.sharding import PartitionSpec as P

HD = 64
epsilon = 1e-05
masked_score = -1e30
gelu_scale = 0.7978845608028654
gelu_cubic = 0.044715


def norm_forward(values, gain, shift):
    average = jnp.mean(values, axis=-1, keepdims=True)
    centered = values - average
    variance = jnp.mean(centered * centered, axis=-1, keepdims=True)
    inverse = lax.rsqrt(variance + epsilon)
    normed = centered * inverse
    return (normed, inverse, normed * gain.astype(jnp.float32) + shift.astype(jnp.float32))


def norm_backward(upstream, normed, inverse, gain):
    scaled = upstream * gain.astype(jnp.float32)
    first_mean = jnp.mean(scaled, axis=-1, keepdims=True)
    second_mean = jnp.mean(scaled * normed, axis=-1, keepdims=True)
    return inverse * (scaled - first_mean - normed * second_mean)


def gelu_pair(pre_act):
    inner_arg = gelu_scale * (pre_act + gelu_cubic * pre_act * pre_act * pre_act)
    tangent = jnp.tanh(inner_arg)
    gelu_value = 0.5 * pre_act * (1.0 + tangent)
    gelu_slope = 0.5 * (1.0 + tangent) + 0.5 * pre_act * (1.0 - tangent * tangent) * gelu_scale * (
        1.0 + 3.0 * gelu_cubic * pre_act * pre_act
    )
    return (gelu_value, gelu_slope)


def shards(
    inputs,
    segment_ids,
    gains,
    shifts,
    attend_weight,
    merge_weight,
    expand_weight,
    expand_bias,
    reduce_weight,
    cotangent,
):
    seq_count, group_len, model_width = inputs.shape
    row_count = seq_count * group_len
    full_len = group_len * lax.axis_size("ctx")
    head_scale = HD ** (-0.5)
    gathered = (
        lax.all_gather(attend_weight, ("shard", "ctx"), axis=0, tiled=True),
        lax.all_gather(merge_weight, ("shard", "ctx"), axis=0, tiled=True),
        lax.all_gather(expand_weight, ("shard", "ctx"), axis=0, tiled=True),
        lax.all_gather(reduce_weight, ("shard", "ctx"), axis=0, tiled=True),
        lax.all_gather(expand_bias, ("shard", "ctx"), axis=1, tiled=True),
        lax.all_gather(gains, ("shard", "ctx"), axis=1, tiled=True),
        lax.all_gather(shifts, ("shard", "ctx"), axis=1, tiled=True),
    )
    attend_full, merge_full, expand_full, reduce_full, bias_full, gains_full, shifts_full = gathered
    local_cols = attend_full.shape[2]
    head_local = local_cols // HD
    flat_in = inputs.reshape(row_count, model_width)
    normed_early, inverse_early, affine_early = norm_forward(flat_in, gains_full[0], shifts_full[0])
    hidden_early = affine_early.astype(jnp.bfloat16)
    projected = jnp.einsum(
        "rd,dtc->rtc", hidden_early, attend_full, preferred_element_type=jnp.float32
    )
    query_heads = (
        (projected[:, 0] * head_scale)
        .astype(jnp.bfloat16)
        .reshape(seq_count, group_len, head_local, HD)
    )
    key_rows = projected[:, 1].astype(jnp.bfloat16).reshape(seq_count, group_len, local_cols)
    value_rows = projected[:, 2].astype(jnp.bfloat16).reshape(seq_count, group_len, local_cols)
    all_keys, all_values, all_segments = (
        lax.all_gather(key_rows, "ctx", axis=1, tiled=True),
        lax.all_gather(value_rows, "ctx", axis=1, tiled=True),
        lax.all_gather(segment_ids, "ctx", axis=1, tiled=True),
    )
    key_heads = all_keys.reshape(seq_count, full_len, head_local, HD)
    value_heads = all_values.reshape(seq_count, full_len, head_local, HD)
    query_pos = lax.axis_index("ctx") * group_len + jnp.arange(group_len, dtype=jnp.int32)
    key_pos = jnp.arange(full_len, dtype=jnp.int32)
    allowed = (segment_ids[:, :, None] == all_segments[:, None, :]) & (
        key_pos[None, None, :] <= query_pos[None, :, None]
    )
    allowed = allowed[:, None]

    def score_block():
        raw_scores = jnp.einsum(
            "sqhd,skhd->shqk", query_heads, key_heads, preferred_element_type=jnp.float32
        )
        return jnp.where(allowed, raw_scores, masked_score)

    scores = score_block()
    row_top = jnp.max(scores, axis=-1, keepdims=True)
    log_total = row_top + jnp.log(jnp.sum(jnp.exp(scores - row_top), axis=-1, keepdims=True))
    attn_probs = jnp.exp(scores - log_total)
    probs_half = attn_probs.astype(jnp.bfloat16)
    attended_heads = jnp.einsum(
        "shqk,skhd->sqhd", probs_half, value_heads, preferred_element_type=jnp.float32
    ).astype(jnp.bfloat16)
    attended = attended_heads.reshape(row_count, local_cols)
    merge_part = jnp.einsum("rc,oc->ro", attended, merge_full, preferred_element_type=jnp.float32)
    residual = flat_in + lax.psum(merge_part, "tp")
    normed_later, inverse_later, affine_later = norm_forward(
        residual, gains_full[1], shifts_full[1]
    )
    hidden_later = affine_later.astype(jnp.bfloat16)
    pre_act = jnp.dot(
        hidden_later, expand_full, preferred_element_type=jnp.float32
    ) + bias_full.astype(jnp.float32)
    gelu_value, gelu_slope = gelu_pair(pre_act)
    activated = gelu_value.astype(jnp.bfloat16)
    reduce_part = jnp.einsum(
        "rf,of->ro", activated, reduce_full, preferred_element_type=jnp.float32
    )
    block_out = residual + lax.psum(reduce_part.astype(jnp.bfloat16), "tp").astype(jnp.float32)
    back_set = (
        lax.all_gather(attend_weight, ("shard", "ctx"), axis=0, tiled=True),
        lax.all_gather(merge_weight, ("shard", "ctx"), axis=0, tiled=True),
        lax.all_gather(expand_weight, ("shard", "ctx"), axis=0, tiled=True),
        lax.all_gather(reduce_weight, ("shard", "ctx"), axis=0, tiled=True),
        lax.all_gather(gains, ("shard", "ctx"), axis=1, tiled=True),
    )
    attend_back, merge_back, expand_back, reduce_back, gains_back = back_set
    output_grad = cotangent.reshape(row_count, model_width)
    cot_half = output_grad.astype(jnp.bfloat16)
    reduce_grad = jnp.einsum("ro,rf->of", cot_half, activated, preferred_element_type=jnp.float32)
    pre_grad = jnp.dot(cot_half, reduce_back, preferred_element_type=jnp.float32) * gelu_slope
    pre_half = pre_grad.astype(jnp.bfloat16)
    bias_grad = jnp.sum(pre_grad, axis=0, keepdims=True)
    expand_grad = jnp.einsum(
        "rd,rf->df", hidden_later, pre_half, preferred_element_type=jnp.float32
    )
    later_part = jnp.einsum("rf,df->rd", pre_half, expand_back, preferred_element_type=jnp.float32)
    later_grad = lax.psum(later_part, "tp")
    residual_grad = output_grad + norm_backward(
        later_grad, normed_later, inverse_later, gains_back[1]
    )
    resid_half = residual_grad.astype(jnp.bfloat16)
    merge_grad = jnp.einsum("ro,rc->oc", resid_half, attended, preferred_element_type=jnp.float32)
    attended_grad = jnp.dot(resid_half, merge_back, preferred_element_type=jnp.float32).astype(
        jnp.bfloat16
    )
    grad_heads = attended_grad.reshape(seq_count, group_len, head_local, HD)
    scores_again = score_block()
    probs_again = jnp.exp(scores_again - log_total)
    probs_again_half = probs_again.astype(jnp.bfloat16)
    row_delta = jnp.einsum(
        "sqhd,sqhd->shq", grad_heads, attended_heads, preferred_element_type=jnp.float32
    )
    prob_grad = jnp.einsum(
        "sqhd,skhd->shqk", grad_heads, value_heads, preferred_element_type=jnp.float32
    )
    score_grad = probs_again * (prob_grad - row_delta[..., None])
    score_half = score_grad.astype(jnp.bfloat16)
    query_grad = (
        jnp.einsum("shqk,skhd->sqhd", score_half, key_heads, preferred_element_type=jnp.float32)
        * head_scale
    )
    keys_part = jnp.einsum(
        "shqk,sqhd->skhd", score_half, query_heads, preferred_element_type=jnp.float32
    ).reshape(seq_count, full_len, local_cols)
    values_part = jnp.einsum(
        "shqk,sqhd->skhd", probs_again_half, grad_heads, preferred_element_type=jnp.float32
    ).reshape(seq_count, full_len, local_cols)
    keys_grad, values_grad = (
        lax.psum_scatter(keys_part, "ctx", scatter_dimension=1, tiled=True),
        lax.psum_scatter(values_part, "ctx", scatter_dimension=1, tiled=True),
    )
    proj_grad = jnp.stack(
        [
            query_grad.reshape(row_count, local_cols),
            keys_grad.reshape(row_count, local_cols),
            values_grad.reshape(row_count, local_cols),
        ],
        axis=1,
    ).astype(jnp.bfloat16)
    attend_grad = jnp.einsum(
        "rd,rtc->dtc", hidden_early, proj_grad, preferred_element_type=jnp.float32
    )
    early_part = jnp.einsum(
        "rtc,dtc->rd", proj_grad, attend_back, preferred_element_type=jnp.float32
    )
    early_grad = lax.psum(early_part, "tp")
    input_grad = residual_grad + norm_backward(
        early_grad, normed_early, inverse_early, gains_back[0]
    )
    gains_grad = jnp.stack(
        [jnp.sum(early_grad * normed_early, axis=0), jnp.sum(later_grad * normed_later, axis=0)]
    )
    shifts_grad = jnp.stack([jnp.sum(early_grad, axis=0), jnp.sum(later_grad, axis=0)])
    shares = (
        lax.psum_scatter(attend_grad, ("shard", "ctx"), scatter_dimension=0, tiled=True),
        lax.psum_scatter(merge_grad, ("shard", "ctx"), scatter_dimension=0, tiled=True),
        lax.psum_scatter(expand_grad, ("shard", "ctx"), scatter_dimension=0, tiled=True),
        lax.psum_scatter(reduce_grad, ("shard", "ctx"), scatter_dimension=0, tiled=True),
        lax.psum_scatter(bias_grad, ("shard", "ctx"), scatter_dimension=1, tiled=True),
        lax.psum_scatter(gains_grad, ("shard", "ctx"), scatter_dimension=1, tiled=True),
        lax.psum_scatter(shifts_grad, ("shard", "ctx"), scatter_dimension=1, tiled=True),
    )
    return (
        block_out.reshape(inputs.shape),
        input_grad.reshape(inputs.shape),
        shares[5],
        shares[6],
        shares[0],
        shares[1],
        shares[2],
        shares[4],
        shares[3],
    )


def solution(mesh):
    in_specs = (
        P("shard", "ctx", None),
        P("shard", "ctx"),
        P(None, ("shard", "ctx")),
        P(None, ("shard", "ctx")),
        P(("shard", "ctx"), None, "tp"),
        P(("shard", "ctx"), "tp"),
        P(("shard", "ctx"), "tp"),
        P("tp", ("shard", "ctx")),
        P(("shard", "ctx"), "tp"),
        P("shard", "ctx", None),
    )
    out_specs = (
        P("shard", "ctx", None),
        P("shard", "ctx", None),
        P(None, ("shard", "ctx")),
        P(None, ("shard", "ctx")),
        P(("shard", "ctx"), None, "tp"),
        P(("shard", "ctx"), "tp"),
        P(("shard", "ctx"), "tp"),
        P("tp", ("shard", "ctx")),
        P(("shard", "ctx"), "tp"),
    )
    return jax.shard_map(shards, mesh=mesh, in_specs=in_specs, out_specs=out_specs, check_vma=False)
```

profile of v0, /device:TPU:0, one launch (start us, length us, event | category | flops | bytes accessed | tf_op | source)
XLA Modules:
  0.0 930.5 jit_solution(1876446625818564370)
XLA Ops:
  9.4 5.5 all_gather.39
  14.8 21.4 %all_gather.35 = bf16[2,1024]{1,0:T(2,128)(2,1)S(1)} all-gather(bf16[2,128]{1,0:T(2,128)(2,1)} %param.12), channel_id=1, replica_groups=mesh['shard'=4,'ctx'=2,'tp'=4] {'shard','ctx'}, dimensions={1}, use_global_device_ids=true | all-gather | bytes 4608 | tf_op jit(solution)/shard_map/all_gather | solution.py:61
  36.3 16.5 %all_gather.36 = bf16[2,1024]{1,0:T(2,128)(2,1)S(1)} all-gather(bf16[2,128]{1,0:T(2,128)(2,1)} %param.13), channel_id=1, replica_groups=mesh['shard'=4,'ctx'=2,'tp'=4] {'shard','ctx'}, dimensions={1}, use_global_device_ids=true | all-gather | bytes 4608 | tf_op jit(solution)/shard_map/all_gather | solution.py:62
  54.6 31.4 %all_gather.41 = bf16[1024,256]{1,0:T(8,128)(2,1)S(1)} all-gather(bf16[128,256]{1,0:T(8,128)(2,1)S(1)} %copy-done.16), channel_id=1, replica_groups=mesh['shard'=4,'ctx'=2,'tp'=4] {'shard','ctx'}, dimensions={0}, use_global_device_ids=true | all-gather | bytes 589824 | tf_op jit(solution)/shard_map/all_gather | solution.py:57
  88.5 5.6 all_gather.38
  95.0 5.6 all_gather.40
  105.7 18.4 %all_gather.43 = bf16[1,1024]{1,0:T(2,128)(2,1)S(1)} all-gather(bf16[1,128]{1,0:T(2,128)(2,1)S(1)} %copy-done.31), channel_id=1, replica_groups=mesh['shard'=4,'ctx'=2,'tp'=4] {'shard','ctx'}, dimensions={1}, use_global_device_ids=true | all-gather | bytes 2304 | tf_op jit(solution)/shard_map/all_gather | solution.py:60
  126.3 13.4 %all-reduce.5.cloned.1.call-done = f32[256,1024]{1,0:T(8,128)} async-done(((f32[256,1024]{1,0:T(8,128)}), f32[256,1024]{1,0:T(8,128)}) %all-reduce.5.cloned.1.call-update) | async-done | bytes 1048592 | tf_op jit(solution)/shard_map/psum | solution.py:110
  141.3 50.0 %all-gather.6.cloned.1.call-done = bf16[1024,1024]{1,0:T(8,128)(2,1)} async-done(((bf16[128,1024]{1,0:T(8,128)(2,1)}), bf16[1024,1024]{1,0:T(8,128)(2,1)}) %all-gather.6.cloned.1.call-update) | async-done | bytes 2097168 | tf_op jit(solution)/shard_map/all_gather | solution.py:58
  191.4 3.3 convolution_add_fusion
  194.7 46.3 %all-gather.8.cloned.1.call-done = bf16[1024,1024]{1,0:T(8,128)(2,1)} async-done(((bf16[128,1024]{1,0:T(8,128)(2,1)}), bf16[1024,1024]{1,0:T(8,128)(2,1)}) %all-gather.8.cloned.1.call-update) | async-done | bytes 2097168 | tf_op jit(solution)/shard_map/all_gather | solution.py:59
  241.0 3.9 fusion.40
  247.5 3.5 convolution_convert_fusion
  251.1 31.3 %all-reduce.9.cloned.1.call-done = f32[256,1024]{1,0:T(8,128)} async-done(((f32[256,1024]{1,0:T(8,128)}), f32[256,1024]{1,0:T(8,128)}) %all-reduce.9.cloned.1.call-update) | async-done | bytes 1048592 | tf_op jit(solution)/shard_map/psum | solution.py:142
  282.4 2.3 multiply_reduce_fusion
  284.8 34.3 %all-reduce.7.cloned.1.call-done = bf16[256,1024]{1,0:T(8,128)(2,1)} async-done(((bf16[256,1024]{1,0:T(8,128)(2,1)}), bf16[256,1024]{1,0:T(8,128)(2,1)}) %all-reduce.7.cloned.1.call-update) | async-done | bytes 524304 | tf_op jit(solution)/shard_map/psum | solution.py:123
  319.1 3.0 bitcast_add_fusion
  332.5 8.7 reduce-scatter.18.cloned.1.call-done
  342.3 15.8 %reduce-scatter.16.cloned.1.call-done = f32[2,128,256]{1,2,0:T(8,128)} async-done(((f32[2,256,256]{1,2,0:T(8,128)}), f32[2,128,256]{1,2,0:T(8,128)}) %reduce-scatter.16.cloned.1.call-update) | async-done | bytes 262160 | tf_op jit(solution)/shard_map/reduce_scatter | solution.py:174
  359.2 3.0 convolution_bitcast_fusion.1
  363.6 35.1 %all-reduce.11.cloned.1.call-done = f32[256,1024]{1,0:T(8,128)} async-done(((f32[256,1024]{1,0:T(8,128)}), f32[256,1024]{1,0:T(8,128)}) %all-reduce.11.cloned.1.call-update) | async-done | bytes 1048592 | tf_op jit(solution)/shard_map/psum | solution.py:191
  398.7 2.5 multiply_reduce_fusion.1
  406.7 3.9 convolution_bitcast_fusion
  414.1 3.4 fusion.11
  418.2 3.9 fusion.19
  422.2 42.8 %reduce-scatter.32.cloned.1.call-done = f32[128,1]{1,0:T(8,128)} async-done(((f32[1024,1]{1,0:T(8,128)}), f32[128,1]{1,0:T(8,128)}) %reduce-scatter.32.cloned.1.call-update) | async-done | bytes 528
  467.8 62.1 %reduce-scatter.30.cloned.1.call-done = f32[128,2]{1,0:T(8,128)} async-done(((f32[1024,2]{1,0:T(8,128)}), f32[128,2]{1,0:T(8,128)}) %reduce-scatter.30.cloned.1.call-update) | async-done | bytes 1040
  531.4 63.9 %reduce-scatter.28.cloned.1.call-done = f32[128,2]{1,0:T(8,128)} async-done(((f32[1024,2]{1,0:T(8,128)}), f32[128,2]{1,0:T(8,128)}) %reduce-scatter.28.cloned.1.call-update) | async-done | bytes 1040
  596.8 89.8 %reduce-scatter.26.cloned.1.call-done = f32[128,1024]{0,1:T(8,128)} async-done(((f32[1024,1024]{0,1:T(8,128)}), f32[128,1024]{0,1:T(8,128)}) %reduce-scatter.26.cloned.1.call-update) | async-done | bytes 524304 | tf_op jit(solution)/shard_map/reduce_scatter | solution.py:203
  688.7 65.8 %reduce-scatter.22.cloned.1.call-done = f32[128,256]{1,0:T(8,128)} async-done(((f32[1024,256]{1,0:T(8,128)}), f32[128,256]{1,0:T(8,128)}) %reduce-scatter.22.cloned.1.call-update) | async-done | bytes 131088 | tf_op jit(solution)/shard_map/reduce_scatter | solution.py:201
  754.5 78.0 %reduce-scatter.20.cloned.1.call-done = f32[128,3,256]{2,0,1:T(8,128)} async-done(((f32[1024,3,256]{2,0,1:T(8,128)}), f32[128,3,256]{2,0,1:T(8,128)}) %reduce-scatter.20.cloned.1.call-update) | async-done | bytes 393232 | tf_op jit(solution)/shard_map/reduce_scatter | solution.py:200
  832.4 91.5 %reduce-scatter.24.cloned.1.call-done = f32[128,1024]{1,0:T(8,128)} async-done(((f32[1024,1024]{1,0:T(8,128)}), f32[128,1024]{1,0:T(8,128)}) %reduce-scatter.24.cloned.1.call-update) | async-done | bytes 524304 | tf_op jit(solution)/shard_map/reduce_scatter | solution.py:202
  (156 shorter events, 49.8 us)
Async XLA Ops:
  7.2 78.8 %copy-start = (f32[2,128,1024]{2,1,0:T(8,128)S(1)}, f32[2,128,1024]{2,1,0:T(8,128)}, u32[]{:S(2)}) copy-start(f32[2,128,1024]{2,1,0:T(8,128)} %param.10) | copy-start | bytes 3145732
  7.2 47.3 %copy-start.28 = (s32[2,128]{1,0:T(2,128)S(1)}, s32[2,128]{1,0:T(2,128)}, u32[]{:S(2)}) copy-start(s32[2,128]{1,0:T(2,128)} %param.11) | copy-start | bytes 3076
  7.2 47.4 %copy-start.16 = (bf16[128,256]{1,0:T(8,128)(2,1)S(1)}, bf16[128,256]{1,0:T(8,128)(2,1)}, u32[]{:S(2)}) copy-start(bf16[128,256]{1,0:T(8,128)(2,1)} %param.15) | copy-start | bytes 196612
  7.2 79.1 %all-gather.4.cloned.1.call-start = ((), (), s32[]{:S(2)}) async-start(), calls=%async_computation.9 | async-start | bytes 1769472 | tf_op jit(solution)/shard_map/all_gather | solution.py:56
  7.9 131.7 %all-reduce.5.cloned.1.call-start = ((), (), s32[]{:S(2)}) async-start(), calls=%async_computation.10 | async-start | bytes 2097152 | tf_op jit(solution)/shard_map/psum | solution.py:110
  52.8 35.6 %copy-start.21 = (f32[256]{0:T(256)}, f32[256]{0:T(256)S(1)}, u32[]{:S(2)}) copy-start(f32[256]{0:T(256)S(1)} %get-tuple-element.54) | copy-start | bytes 3076
  54.3 34.1 %copy-start.23 = (f32[256]{0:T(256)}, f32[256]{0:T(256)S(1)}, u32[]{:S(2)}) copy-start(f32[256]{0:T(256)S(1)} %rsqrt_bitcast_fusion) | copy-start | bytes 3076
  54.4 137.0 %copy-start.19 = (f32[1,1024]{1,0:T(1,128)}, f32[1,1024]{1,0:T(1,128)S(1)}, u32[]{:S(2)}) copy-start(f32[1,1024]{1,0:T(1,128)S(1)} %get-tuple-element.52) | copy-start | bytes 12292
  86.0 16.5 %copy-start.3 = (bf16[1024,256]{1,0:T(8,128)(2,1)}, bf16[1024,256]{1,0:T(8,128)(2,1)S(1)}, u32[]{:S(2)}) copy-start(bf16[1024,256]{1,0:T(8,128)(2,1)S(1)} %all_gather.41) | copy-start | bytes 1572868
  102.5 23.8 %copy-start.14 = (bf16[2,128,4,64]{1,0,3,2:T(2,128)(2,1)}, bf16[2,128,4,64]{1,0,3,2:T(2,128)(2,1)S(1)}, u32[]{:S(2)}) copy-start(bf16[2,128,4,64]{1,0,3,2:T(2,128)(2,1)S(1)} %copy.48) | copy-start | bytes 393220
  104.3 87.0 %all-gather.6.cloned.1.call-start = ((), (), s32[]{:S(2)}) async-start(), calls=%async_computation.11 | async-start | bytes 2359296 | tf_op jit(solution)/shard_map/all_gather | solution.py:58
  105.1 135.9 %all-gather.8.cloned.1.call-start = ((), (), s32[]{:S(2)}) async-start(), calls=%async_computation.12 | async-start | bytes 2359296 | tf_op jit(solution)/shard_map/all_gather | solution.py:59
  105.7 176.8 %all-reduce.9.cloned.1.call-start = ((), (), s32[]{:S(2)}) async-start(), calls=%async_computation.14 | async-start | bytes 2097152 | tf_op jit(solution)/shard_map/psum | solution.py:142
  141.3 177.8 %copy-start.25 = (f32[256]{0:T(256)}, f32[256]{0:T(256)S(1)}, u32[]{:S(2)}) copy-start(f32[256]{0:T(256)S(1)} %add_rsqrt_fusion) | copy-start | bytes 3076
  247.5 71.6 %all-reduce.7.cloned.1.call-start = ((), (), s32[]{:S(2)}) async-start(), calls=%async_computation.13 | async-start | bytes 1048576 | tf_op jit(solution)/shard_map/psum | solution.py:123
  251.1 90.2 %reduce-scatter.18.cloned.1.call-start = ((), (), s32[]{:S(2)}) async-start(), calls=%async_computation.16 | async-start | bytes 786432 | tf_op jit(solution)/shard_map/reduce_scatter | solution.py:175
  326.3 31.8 %reduce-scatter.16.cloned.1.call-start = ((), (), s32[]{:S(2)}) async-start(), calls=%async_computation.15 | async-start | bytes 786432 | tf_op jit(solution)/shard_map/reduce_scatter | solution.py:174
  330.7 68.0 %all-reduce.11.cloned.1.call-start = ((), (), s32[]{:S(2)}) async-start(), calls=%async_computation.17 | async-start | bytes 2097152 | tf_op jit(solution)/shard_map/psum | solution.py:191
  362.3 102.8 %reduce-scatter.32.cloned.1.call-start = ((), (), s32[]{:S(2)}) async-start(), calls=%async_computation.24 | async-start | bytes 589824
  362.3 41.3 %copy-start.17 = (f32[1024]{0:T(1024)S(1)}, f32[1024]{0:T(1024)}, u32[]{:S(2)}) copy-start(f32[1024]{0:T(1024)} %get-tuple-element.38) | copy-start | bytes 12292
  363.4 43.3 %copy-start.8 = (f32[256,1024]{1,0:T(8,128)S(1)}, f32[256,1024]{1,0:T(8,128)}, u32[]{:S(2)}) copy-start(f32[256,1024]{1,0:T(8,128)} %convolution_add_fusion) | copy-start | bytes 3145732
  363.4 166.6 %reduce-scatter.30.cloned.1.call-start = ((), (), s32[]{:S(2)}) async-start(), calls=%async_computation.23 | async-start | bytes 589824
  403.5 191.8 %reduce-scatter.28.cloned.1.call-start = ((), (), s32[]{:S(2)}) async-start(), calls=%async_computation.22 | async-start | bytes 589824
  406.6 280.0 %reduce-scatter.26.cloned.1.call-start = ((), (), s32[]{:S(2)}) async-start(), calls=%async_computation.21 | async-start | bytes 4718592 | tf_op jit(solution)/shard_map/reduce_scatter | solution.py:203
  410.6 343.9 %reduce-scatter.22.cloned.1.call-start = ((), (), s32[]{:S(2)}) async-start(), calls=%async_computation.19 | async-start | bytes 1179648 | tf_op jit(solution)/shard_map/reduce_scatter | solution.py:201
  414.1 418.3 %reduce-scatter.20.cloned.1.call-start = ((), (), s32[]{:S(2)}) async-start(), calls=%async_computation.18 | async-start | bytes 3538944 | tf_op jit(solution)/shard_map/reduce_scatter | solution.py:200
  417.6 506.4 %reduce-scatter.24.cloned.1.call-start = ((), (), s32[]{:S(2)}) async-start(), calls=%async_computation.20 | async-start | bytes 4718592 | tf_op jit(solution)/shard_map/reduce_scatter | solution.py:202
  422.1 44.3 %copy-start.30 = (f32[256]{0:T(256)S(1)}, f32[256]{0:T(256)}, u32[]{:S(2)}) copy-start(f32[256]{0:T(256)} %get-tuple-element.37) | copy-start | bytes 3076
  422.1 44.3 %copy-start.29 = (f32[256]{0:T(256)S(1)}, f32[256]{0:T(256)}, u32[]{:S(2)}) copy-start(f32[256]{0:T(256)} %get-tuple-element.41) | copy-start | bytes 3076
  422.1 44.3 %copy-start.7 = (f32[256,1024]{1,0:T(8,128)S(1)}, f32[256,1024]{1,0:T(8,128)}, u32[]{:S(2)}) copy-start(f32[256,1024]{1,0:T(8,128)} %all-reduce.11.cloned.1.call-done) | copy-start | bytes 3145732
  422.1 44.3 %copy-start.22 = (f32[256]{0:T(256)S(1)}, f32[256]{0:T(256)}, u32[]{:S(2)}) copy-start(f32[256]{0:T(256)} %copy-done.21) | copy-start | bytes 3076
  422.1 44.4 %copy-start.24 = (f32[256]{0:T(256)S(1)}, f32[256]{0:T(256)}, u32[]{:S(2)}) copy-start(f32[256]{0:T(256)} %copy-done.23) | copy-start | bytes 3076
  (16 other events, 37.4 us)
Sparse Core Ops, SparseCore 0:
  10.2 47.6 all-gather.3
  104.5 35.1 all-reduce.4
  141.8 49.5 all-gather.5
  193.3 47.6 all-gather.7
  247.6 34.8 all-reduce.8
  285.2 33.8 all-reduce.6
  326.5 14.7 reduce-scatter.17
  343.5 14.6 reduce-scatter.15
  362.4 36.2 all-reduce.10
  401.9 63.0 reduce-scatter.31
  468.4 61.5 reduce-scatter.29
  533.7 61.5 reduce-scatter.27
  599.0 87.6 reduce-scatter.25
  690.5 63.9 reduce-scatter.21
  758.5 73.8 reduce-scatter.19
  836.5 87.4 reduce-scatter.23
where the time goes:
time: 932 us; the launch traced here: 930 us
  waiting for transfers between devices  731 us (78%)
  blocking collectives  105 us (11%)
  matrix products  38.5 us (4%)
  other arithmetic  21.5 us (2%)
  local copies, waits for them, and re-layouts  19.6 us (2%)
  between operations  14.5 us (2%)
    unnamed x19, waiting for transfers between devices  171 us
    reduce_scatter x1, waiting for transfers between devices, shards(): lax.psum_scatter(expand_grad, ('shard', 'ctx'), scatter_dimension=0, tile...  91.5 us
    reduce_scatter x1, waiting for transfers between devices, shards(): lax.psum_scatter(reduce_grad, ('shard', 'ctx'), scatter_dimension=0, tile...  89.8 us
    reduce_scatter x1, waiting for transfers between devices, shards(): lax.psum_scatter(attend_grad, ('shard', 'ctx'), scatter_dimension=0, tile...  78 us
    reduce_scatter x1, waiting for transfers between devices, shards(): lax.psum_scatter(merge_grad, ('shard', 'ctx'), scatter_dimension=0, tiled...  65.8 us
    all_gather x1, waiting for transfers between devices, shards(): lax.all_gather(expand_weight, ('shard', 'ctx'), axis=0, tiled=True)  50 us
    all_gather x1, waiting for transfers between devices, shards(): lax.all_gather(reduce_weight, ('shard', 'ctx'), axis=0, tiled=True)  46.3 us
    psum x1, waiting for transfers between devices, shards(): early_grad = lax.psum(early_part, 'tp')  35.1 us
  transfers between devices with their start and end apart: 16, of which 15 were waited for; matrix products, arithmetic and copies ran while one was open for 6% of the time, Pallas kernels for 0%

commit v1 on v0

--- a/solution.py
+++ b/solution.py
@@ -139,7 +139,11 @@
         "rd,rf->df", hidden_later, pre_half, preferred_element_type=jnp.float32
     )
     later_part = jnp.einsum("rf,df->rd", pre_half, expand_back, preferred_element_type=jnp.float32)
-    later_grad = lax.psum(later_part, "tp")
+    later_grad = later_part
+    for hop in (1, 2):
+        later_grad = later_grad + lax.ppermute(
+            later_grad, "tp", [(dev, dev ^ hop) for dev in range(4)]
+        )
     residual_grad = output_grad + norm_backward(
         later_grad, normed_later, inverse_later, gains_back[1]
     )

time: 932 us -> 899 us (0.965)
  waiting for transfers between devices: 731 us -> 698 us
    psum x1, waiting for transfers between devices: 34.3 us -> 1.39 us  [shards(): lax.psum(reduce_part.astype(jnp.bfloat16), 'tp').astype(jnp.float32)]
    ppermute x0 -> x2, waiting for transfers between devices: none -> 31.4 us  [shards(): lax.ppermute(later_grad, 'tp', [(dev, dev ^ hop) for dev in range(4)])]
    psum x1 -> x0, waiting for transfers between devices: 31.3 us -> none  [shards(): later_grad = lax.psum(later_part, 'tp')]
    unnamed x19 -> x18, waiting for transfers between devices: 171 us -> 171 us
  transfers between devices with their start and end apart: 16 -> 17, of which waited for: 15 -> 16; matrix products, arithmetic and copies ran while one was open for 6% -> 6% of each run, Pallas kernels for 0% -> 0%
where the time goes in v1:
time: 899 us; the launch traced here: 898 us
  waiting for transfers between devices  698 us (78%)
  blocking collectives  105 us (12%)
  matrix products  34.6 us (4%)
  other arithmetic  24.4 us (3%)
  local copies, waits for them, and re-layouts  19.1 us (2%)
  between operations  14.5 us (2%)
    unnamed x18, waiting for transfers between devices  171 us
    reduce_scatter x1, waiting for transfers between devices, shards(): lax.psum_scatter(expand_grad, ('shard', 'ctx'), scatter_dimension=0, tile...  91.5 us
    reduce_scatter x1, waiting for transfers between devices, shards(): lax.psum_scatter(reduce_grad, ('shard', 'ctx'), scatter_dimension=0, tile...  89.7 us
    reduce_scatter x1, waiting for transfers between devices, shards(): lax.psum_scatter(attend_grad, ('shard', 'ctx'), scatter_dimension=0, tile...  78.7 us
    reduce_scatter x1, waiting for transfers between devices, shards(): lax.psum_scatter(merge_grad, ('shard', 'ctx'), scatter_dimension=0, tiled...  65.8 us
    all_gather x1, waiting for transfers between devices, shards(): lax.all_gather(expand_weight, ('shard', 'ctx'), axis=0, tiled=True)  50 us
    all_gather x1, waiting for transfers between devices, shards(): lax.all_gather(reduce_weight, ('shard', 'ctx'), axis=0, tiled=True)  46.3 us
    psum x1, waiting for transfers between devices, shards(): early_grad = lax.psum(early_part, 'tp')  35.1 us
  transfers between devices with their start and end apart: 17, of which 16 were waited for; matrix products, arithmetic and copies ran while one was open for 6% of the time, Pallas kernels for 0%

profile of v1, /device:TPU:0, one launch (start us, length us, event | category | flops | bytes accessed | tf_op | source)
XLA Modules:
  0.0 897.9 jit_solution(10303882214956776308)
XLA Ops:
  9.4 5.5 all_gather.39
  14.8 21.4 %all_gather.35 = bf16[2,1024]{1,0:T(2,128)(2,1)S(1)} all-gather(bf16[2,128]{1,0:T(2,128)(2,1)} %param.12), channel_id=1, replica_groups=mesh['shard'=4,'ctx'=2,'tp'=4] {'shard','ctx'}, dimensions={1}, use_global_device_ids=true | all-gather | bytes 4608 | tf_op jit(solution)/shard_map/all_gather | solution.py:61
  36.3 16.5 %all_gather.36 = bf16[2,1024]{1,0:T(2,128)(2,1)S(1)} all-gather(bf16[2,128]{1,0:T(2,128)(2,1)} %param.13), channel_id=1, replica_groups=mesh['shard'=4,'ctx'=2,'tp'=4] {'shard','ctx'}, dimensions={1}, use_global_device_ids=true | all-gather | bytes 4608 | tf_op jit(solution)/shard_map/all_gather | solution.py:62
  54.6 31.4 %all_gather.41 = bf16[1024,256]{1,0:T(8,128)(2,1)S(1)} all-gather(bf16[128,256]{1,0:T(8,128)(2,1)S(1)} %copy-done.18), channel_id=1, replica_groups=mesh['shard'=4,'ctx'=2,'tp'=4] {'shard','ctx'}, dimensions={0}, use_global_device_ids=true | all-gather | bytes 589824 | tf_op jit(solution)/shard_map/all_gather | solution.py:57
  88.5 5.6 all_gather.38
  95.0 5.6 all_gather.40
  105.7 18.4 %all_gather.43 = bf16[1,1024]{1,0:T(2,128)(2,1)S(1)} all-gather(bf16[1,128]{1,0:T(2,128)(2,1)S(1)} %copy-done.30), channel_id=1, replica_groups=mesh['shard'=4,'ctx'=2,'tp'=4] {'shard','ctx'}, dimensions={1}, use_global_device_ids=true | all-gather | bytes 2304 | tf_op jit(solution)/shard_map/all_gather | solution.py:60
  126.3 13.4 %all-reduce.4.cloned.1.call-done = f32[256,1024]{1,0:T(8,128)} async-done(((f32[256,1024]{1,0:T(8,128)}), f32[256,1024]{1,0:T(8,128)}) %all-reduce.4.cloned.1.call-update) | async-done | bytes 1048592 | tf_op jit(solution)/shard_map/psum | solution.py:110
  141.3 50.0 %all-gather.6.cloned.1.call-done = bf16[1024,1024]{1,0:T(8,128)(2,1)} async-done(((bf16[128,1024]{1,0:T(8,128)(2,1)}), bf16[1024,1024]{1,0:T(8,128)(2,1)}) %all-gather.6.cloned.1.call-update) | async-done | bytes 2097168 | tf_op jit(solution)/shard_map/all_gather | solution.py:58
  191.4 3.3 convolution_add_fusion
  194.7 46.3 %all-gather.8.cloned.1.call-done = bf16[1024,1024]{1,0:T(8,128)(2,1)} async-done(((bf16[128,1024]{1,0:T(8,128)(2,1)}), bf16[1024,1024]{1,0:T(8,128)(2,1)}) %all-gather.8.cloned.1.call-update) | async-done | bytes 2097168 | tf_op jit(solution)/shard_map/all_gather | solution.py:59
  241.0 3.9 fusion.40
  245.8 2.6 collective-permute-done
  252.7 28.7 %collective-permute-done.1 = f32[256,1024]{1,0:T(8,128)} collective-permute-done((f32[256,1024]{1,0:T(8,128)}, f32[256,1024]{1,0:T(8,128)}, u32[]{:S(2)}, u32[]{:S(2)}) %collective-permute-start.1) | collective-permute-done | bytes 1048608 | tf_op jit(solution)/shard_map/ppermute | solution.py:144
  281.5 3.5 multiply_reduce_fusion
  286.4 3.0 bitcast_add_fusion
  299.8 8.2 reduce-scatter.18.cloned.1.call-done
  309.1 15.8 %reduce-scatter.16.cloned.1.call-done = f32[2,128,256]{1,2,0:T(8,128)} async-done(((f32[2,256,256]{1,2,0:T(8,128)}), f32[2,128,256]{1,2,0:T(8,128)}) %reduce-scatter.16.cloned.1.call-update) | async-done | bytes 262160 | tf_op jit(solution)/shard_map/reduce_scatter | solution.py:178
  326.1 3.0 convolution_bitcast_fusion.1
  330.4 35.1 %all-reduce.8.cloned.1.call-done = f32[256,1024]{1,0:T(8,128)} async-done(((f32[256,1024]{1,0:T(8,128)}), f32[256,1024]{1,0:T(8,128)}) %all-reduce.8.cloned.1.call-update) | async-done | bytes 1048592 | tf_op jit(solution)/shard_map/psum | solution.py:195
  365.5 2.4 multiply_reduce_fusion.1
  374.1 3.9 convolution_bitcast_fusion
  379.2 2.3 fusion.16
  381.5 3.9 fusion.19
  386.5 2.4 fusion.11
  388.9 43.1 %reduce-scatter.32.cloned.1.call-done = f32[128,1]{1,0:T(8,128)} async-done(((f32[1024,1]{1,0:T(8,128)}), f32[128,1]{1,0:T(8,128)}) %reduce-scatter.32.cloned.1.call-update) | async-done | bytes 528
  434.8 62.0 %reduce-scatter.30.cloned.1.call-done = f32[128,2]{1,0:T(8,128)} async-done(((f32[1024,2]{1,0:T(8,128)}), f32[128,2]{1,0:T(8,128)}) %reduce-scatter.30.cloned.1.call-update) | async-done | bytes 1040
  498.2 64.1 %reduce-scatter.28.cloned.1.call-done = f32[128,2]{1,0:T(8,128)} async-done(((f32[1024,2]{1,0:T(8,128)}), f32[128,2]{1,0:T(8,128)}) %reduce-scatter.28.cloned.1.call-update) | async-done | bytes 1040
  563.8 89.7 %reduce-scatter.26.cloned.1.call-done = f32[128,1024]{0,1:T(8,128)} async-done(((f32[1024,1024]{0,1:T(8,128)}), f32[128,1024]{0,1:T(8,128)}) %reduce-scatter.26.cloned.1.call-update) | async-done | bytes 524304 | tf_op jit(solution)/shard_map/reduce_scatter | solution.py:207
  655.5 65.8 %reduce-scatter.22.cloned.1.call-done = f32[128,256]{1,0:T(8,128)} async-done(((f32[1024,256]{1,0:T(8,128)}), f32[128,256]{1,0:T(8,128)}) %reduce-scatter.22.cloned.1.call-update) | async-done | bytes 131088 | tf_op jit(solution)/shard_map/reduce_scatter | solution.py:205
  721.3 91.5 %reduce-scatter.24.cloned.1.call-done = f32[128,1024]{1,0:T(8,128)} async-done(((f32[1024,1024]{1,0:T(8,128)}), f32[128,1024]{1,0:T(8,128)}) %reduce-scatter.24.cloned.1.call-update) | async-done | bytes 524304 | tf_op jit(solution)/shard_map/reduce_scatter | solution.py:206
  812.7 78.7 %reduce-scatter.20.cloned.1.call-done = f32[128,3,256]{2,0,1:T(8,128)} async-done(((f32[1024,3,256]{2,0,1:T(8,128)}), f32[128,3,256]{2,0,1:T(8,128)}) %reduce-scatter.20.cloned.1.call-update) | async-done | bytes 393232 | tf_op jit(solution)/shard_map/reduce_scatter | solution.py:204
  (158 shorter events, 52.3 us)
Async XLA Ops:
  7.2 78.8 %copy-start = (f32[2,128,1024]{2,1,0:T(8,128)S(1)}, f32[2,128,1024]{2,1,0:T(8,128)}, u32[]{:S(2)}) copy-start(f32[2,128,1024]{2,1,0:T(8,128)} %param.10) | copy-start | bytes 3145732
  7.2 47.3 %copy-start.27 = (s32[2,128]{1,0:T(2,128)S(1)}, s32[2,128]{1,0:T(2,128)}, u32[]{:S(2)}) copy-start(s32[2,128]{1,0:T(2,128)} %param.11) | copy-start | bytes 3076
  7.2 47.4 %copy-start.18 = (bf16[128,256]{1,0:T(8,128)(2,1)S(1)}, bf16[128,256]{1,0:T(8,128)(2,1)}, u32[]{:S(2)}) copy-start(bf16[128,256]{1,0:T(8,128)(2,1)} %param.15) | copy-start | bytes 196612
  7.2 79.1 %all-gather.4.cloned.1.call-start = ((), (), s32[]{:S(2)}) async-start(), calls=%async_computation.9 | async-start | bytes 1769472 | tf_op jit(solution)/shard_map/all_gather | solution.py:56
  7.9 131.7 %all-reduce.4.cloned.1.call-start = ((), (), s32[]{:S(2)}) async-start(), calls=%async_computation.10 | async-start | bytes 2097152 | tf_op jit(solution)/shard_map/psum | solution.py:110
  52.8 35.6 %copy-start.21 = (f32[256]{0:T(256)}, f32[256]{0:T(256)S(1)}, u32[]{:S(2)}) copy-start(f32[256]{0:T(256)S(1)} %get-tuple-element.55) | copy-start | bytes 3076
  54.3 34.1 %copy-start.23 = (f32[256]{0:T(256)}, f32[256]{0:T(256)S(1)}, u32[]{:S(2)}) copy-start(f32[256]{0:T(256)S(1)} %rsqrt_bitcast_fusion) | copy-start | bytes 3076
  54.4 137.0 %copy-start.19 = (f32[1,1024]{1,0:T(1,128)}, f32[1,1024]{1,0:T(1,128)S(1)}, u32[]{:S(2)}) copy-start(f32[1,1024]{1,0:T(1,128)S(1)} %get-tuple-element.53) | copy-start | bytes 12292
  86.0 16.5 %copy-start.3 = (bf16[1024,256]{1,0:T(8,128)(2,1)}, bf16[1024,256]{1,0:T(8,128)(2,1)S(1)}, u32[]{:S(2)}) copy-start(bf16[1024,256]{1,0:T(8,128)(2,1)S(1)} %all_gather.41) | copy-start | bytes 1572868
  102.5 23.7 %copy-start.16 = (bf16[2,128,4,64]{1,0,3,2:T(2,128)(2,1)}, bf16[2,128,4,64]{1,0,3,2:T(2,128)(2,1)S(1)}, u32[]{:S(2)}) copy-start(bf16[2,128,4,64]{1,0,3,2:T(2,128)(2,1)S(1)} %copy.48) | copy-start | bytes 393220
  104.3 87.0 %all-gather.6.cloned.1.call-start = ((), (), s32[]{:S(2)}) async-start(), calls=%async_computation.11 | async-start | bytes 2359296 | tf_op jit(solution)/shard_map/all_gather | solution.py:58
  105.1 135.9 %all-gather.8.cloned.1.call-start = ((), (), s32[]{:S(2)}) async-start(), calls=%async_computation.12 | async-start | bytes 2359296 | tf_op jit(solution)/shard_map/all_gather | solution.py:59
  105.6 180.7 %all-reduce.6.cloned.1.call-start = ((), (), s32[]{:S(2)}) async-start(), calls=%async_computation.13 | async-start | bytes 1048576 | tf_op jit(solution)/shard_map/psum | solution.py:123
  141.3 145.1 %copy-start.25 = (f32[256]{0:T(256)}, f32[256]{0:T(256)S(1)}, u32[]{:S(2)}) copy-start(f32[256]{0:T(256)S(1)} %add_rsqrt_fusion) | copy-start | bytes 3076
  245.7 2.7 collective-permute-start
  249.5 31.9 %collective-permute-start.1 = (f32[256,1024]{1,0:T(8,128)}, f32[256,1024]{1,0:T(8,128)}, u32[]{:S(2)}, u32[]{:S(2)}) collective-permute-start(f32[256,1024]{1,0:T(8,128)} %add.152), channel_id=1, source_target_pairs={{0,2},{1,3},{2,0},{3,1},{4,6},{5,7},{6,4},{7,5},{8,10},{9,11},{10,... | collective-permute-start | bytes 3145736 | tf_op jit(solution)/shard_map/ppermute | solution.py:144
  252.7 55.4 %reduce-scatter.18.cloned.1.call-start = ((), (), s32[]{:S(2)}) async-start(), calls=%async_computation.15 | async-start | bytes 786432 | tf_op jit(solution)/shard_map/reduce_scatter | solution.py:179
  293.6 31.4 %reduce-scatter.16.cloned.1.call-start = ((), (), s32[]{:S(2)}) async-start(), calls=%async_computation.14 | async-start | bytes 786432 | tf_op jit(solution)/shard_map/reduce_scatter | solution.py:178
  298.0 67.5 %all-reduce.8.cloned.1.call-start = ((), (), s32[]{:S(2)}) async-start(), calls=%async_computation.16 | async-start | bytes 2097152 | tf_op jit(solution)/shard_map/psum | solution.py:195
  329.1 102.9 %reduce-scatter.32.cloned.1.call-start = ((), (), s32[]{:S(2)}) async-start(), calls=%async_computation.23 | async-start | bytes 589824
  330.2 43.9 %copy-start.10 = (f32[256,1024]{1,0:T(8,128)S(1)}, f32[256,1024]{1,0:T(8,128)}, u32[]{:S(2)}) copy-start(f32[256,1024]{1,0:T(8,128)} %convolution_add_fusion) | copy-start | bytes 3145732
  330.2 166.6 %reduce-scatter.30.cloned.1.call-start = ((), (), s32[]{:S(2)}) async-start(), calls=%async_computation.22 | async-start | bytes 589824
  370.9 191.4 %reduce-scatter.28.cloned.1.call-start = ((), (), s32[]{:S(2)}) async-start(), calls=%async_computation.21 | async-start | bytes 589824
  374.0 279.4 %reduce-scatter.26.cloned.1.call-start = ((), (), s32[]{:S(2)}) async-start(), calls=%async_computation.20 | async-start | bytes 4718592 | tf_op jit(solution)/shard_map/reduce_scatter | solution.py:207
  378.0 343.3 %reduce-scatter.22.cloned.1.call-start = ((), (), s32[]{:S(2)}) async-start(), calls=%async_computation.18 | async-start | bytes 1179648 | tf_op jit(solution)/shard_map/reduce_scatter | solution.py:205
  381.5 431.2 %reduce-scatter.24.cloned.1.call-start = ((), (), s32[]{:S(2)}) async-start(), calls=%async_computation.19 | async-start | bytes 4718592 | tf_op jit(solution)/shard_map/reduce_scatter | solution.py:206
  385.5 505.9 %reduce-scatter.20.cloned.1.call-start = ((), (), s32[]{:S(2)}) async-start(), calls=%async_computation.17 | async-start | bytes 3538944 | tf_op jit(solution)/shard_map/reduce_scatter | solution.py:204
  388.8 44.5 %copy-start.29 = (f32[256]{0:T(256)S(1)}, f32[256]{0:T(256)}, u32[]{:S(2)}) copy-start(f32[256]{0:T(256)} %get-tuple-element.37) | copy-start | bytes 3076
  388.9 44.5 %copy-start.28 = (f32[256]{0:T(256)S(1)}, f32[256]{0:T(256)}, u32[]{:S(2)}) copy-start(f32[256]{0:T(256)} %get-tuple-element.41) | copy-start | bytes 3076
  388.9 44.6 %copy-start.8 = (f32[256,1024]{1,0:T(8,128)S(1)}, f32[256,1024]{1,0:T(8,128)}, u32[]{:S(2)}) copy-start(f32[256,1024]{1,0:T(8,128)} %all-reduce.8.cloned.1.call-done) | copy-start | bytes 3145732
  388.9 44.6 %copy-start.22 = (f32[256]{0:T(256)S(1)}, f32[256]{0:T(256)}, u32[]{:S(2)}) copy-start(f32[256]{0:T(256)} %copy-done.21) | copy-start | bytes 3076
  388.9 44.6 %copy-start.24 = (f32[256]{0:T(256)S(1)}, f32[256]{0:T(256)}, u32[]{:S(2)}) copy-start(f32[256]{0:T(256)} %copy-done.23) | copy-start | bytes 3076
  (17 other events, 51.9 us)
Sparse Core Ops, SparseCore 0:
  10.2 47.6 all-gather.3
  104.5 35.1 all-reduce.3
  141.8 49.5 all-gather.5
  193.3 47.6 all-gather.7
  252.8 33.5 all-reduce.5
  293.7 14.2 reduce-scatter.17
  310.3 14.6 reduce-scatter.15
  329.2 36.2 all-reduce.7
  368.9 63.0 reduce-scatter.31
  435.1 61.5 reduce-scatter.29
  500.7 61.5 reduce-scatter.27
  565.8 87.6 reduce-scatter.25
  657.4 63.7 reduce-scatter.21
  725.3 87.3 reduce-scatter.23
  816.7 74.5 reduce-scatter.19
